TPU v7x, 32 devices: a whole 2x2x4 slice. The times are simulated.
32 devices in a mesh: rows: 8 (over z, core), pairs: 4 (over y, x).
Axes of the slice: x: 2, y: 2, z: 4, core: 2. Of those that a mesh axis runs over, the one named last changes fastest.
Arguments:
- observed: float32 [12288, 2048], P('rows', 'pairs'), as said below
- estimate: float32 [12288, 2048], P('rows', 'pairs'), may hold values from -0.054126587 to 0.054126587
- mask: int32 [12288, 2048], P('rows', 'pairs'), may hold values from 0 to 1
- threshold: float32 [2048], P('pairs'), may hold values from 0.02 to 0.12
Outputs:
- regrouped: float32 [2048, 12288], P(('rows', 'pairs'))
Inputs may be any that keep to these rules, and one draw needn't show every extreme that they name: observed has entries of order 12288^-1/2.
All inputs are finite; a program needn't handle non-finite values.
Results may differ from a plain program's by a relative error of at most 0.0003.
Values sent between devices are 32-bit elements; how exact they have to be, the bound alone decides.
A program may use at most 128 MiB of HBM per device.

v0:
```python
import jax
import jax.numpy as jnp
from jax import lax
from jax.sharding import PartitionSpec as P

ROUNDS = 4
NS_STEPS = 3
HI = lax.Precision.HIGHEST


def from_behind(block, axis, distance):
    devices = range(lax.axis_size(axis))
    route = [((i - distance) % len(devices), i) for i in devices]
    return lax.ppermute(block, axis, route)


def whitening_of(gram):
    width = gram.shape[-1]
    eye = jnp.eye(width, dtype=jnp.float32)
    dsum = jnp.diagonal(gram, axis1=-2, axis2=-1) + 1e-06
    inv_root = 1.0 / jnp.sqrt(dsum)
    normed = gram * inv_root[..., :, None] * inv_root[..., None, :]
    fro = jnp.sqrt(jnp.sum(normed * normed, axis=(-2, -1)))
    ymat = normed / fro[..., None, None]
    zmat = jnp.broadcast_to(eye, normed.shape)
    for step in range(NS_STEPS):
        tmat = 1.5 * eye - 0.5 * jnp.einsum("pij,pjk->pik", zmat, ymat, precision=HI)
        ymat = jnp.einsum("pij,pjk->pik", ymat, tmat, precision=HI)
        zmat = jnp.einsum("pij,pjk->pik", tmat, zmat, precision=HI)
    return (
        inv_root[..., :, None]
        * zmat
        * jnp.sqrt(dsum)[..., None, :]
        / jnp.sqrt(fro)[..., None, None]
    )


def on_device(observed, estimate, mask, threshold):
    filled = jnp.where(mask == 1, observed, estimate)
    rows_here, width = filled.shape
    block = width // 4
    for round_index in range(ROUNDS):
        pairs = filled.reshape(rows_here, 2, 2 * block)
        partial_gram = jnp.einsum("rpi,rpj->pij", pairs, pairs, precision=HI)
        gram = lax.psum(partial_gram, "rows")
        whitening = whitening_of(gram)
        pairs = jnp.einsum("rpi,pij->rpj", pairs, whitening, precision=HI)
        quads = pairs.reshape(rows_here, 4, block)
        if round_index + 1 < ROUNDS:
            moved = from_behind(quads[:, 3], "pairs", 1)
            quads = jnp.stack([quads[:, 0], moved, quads[:, 2], quads[:, 1]], axis=1)
        filled = quads.reshape(rows_here, width)
    squares = lax.psum(jnp.sum(filled * filled, axis=0), "rows")
    col_norm = jnp.sqrt(squares + 1e-06)
    factor = jnp.maximum(col_norm - threshold, 0.0) / col_norm
    shrunk_t = (filled * factor[None, :]).T
    count_rows = lax.axis_size("rows")
    count_pairs = lax.axis_size("pairs")
    each_dest = width // (count_rows * count_pairs)
    packed = shrunk_t.reshape(count_rows * count_pairs, each_dest, rows_here)
    landed = lax.all_to_all(packed, ("rows", "pairs"), split_axis=0, concat_axis=1, tiled=True)
    landed = landed.reshape(count_rows, count_pairs, each_dest, rows_here).transpose(2, 1, 0, 3)
    return landed.reshape(each_dest * count_pairs, count_rows * rows_here)


def solution(mesh):
    placed = (P("rows", "pairs"), P("rows", "pairs"), P("rows", "pairs"), P("pairs"))
    return jax.shard_map(
        on_device, mesh=mesh, in_specs=placed, out_specs=P(("rows", "pairs"), None), check_vma=False
    )
```

profile of v0, /device:TPU:0, one launch (start us, length us, event | category | flops | bytes accessed | tf_op | source)
XLA Modules:
  0.0 571.2 jit_solution(13144928827066859881)
XLA Ops:
  6.5 4.9 compare_select_fusion
  11.4 6.2 %fusion.2 = f32[2,256,256]{2,1,0:T(8,128)} fusion(f32[192,2,8,256]{3,2,1,0:T(8,128)S(1)} %bitcast.133), kind=kOutput, calls=%fused_computation.6 | convolution fusion | flops 2415919104 | bytes 3670016 | tf_op jit(solution)/shard_map/rpi,rpj->pij/dot_general | solution.py:44
  18.5 58.6 %all-reduce.5.cloned.1.call-done = f32[2,256,256]{2,1,0:T(8,128)} async-done(((f32[2,256,256]{2,1,0:T(8,128)}), f32[2,256,256]{2,1,0:T(8,128)}) %all-reduce.5.cloned.1.call-update) | async-done | bytes 524304 | tf_op jit(solution)/shard_map/psum | solution.py:45
  77.0 17.5 %copy.62 = f32[2,256,256]{0,2,1:T(8,128)} copy(f32[2,256,256]{2,1,0:T(8,128)} %all-reduce.5.cloned.1.call-done) | data formatting | bytes 1048576 | tf_op jit(solution)/shard_map/psum | solution.py:45
  94.5 3.0 gather_fusion
  101.5 1.9 fusion.26
  112.0 5.3 fusion
  119.1 16.9 %collective-permute-done = f32[1536,128]{0,1:T(8,128)S(1)} collective-permute-done((f32[1536,128]{0,1:T(8,128)S(1)}, f32[1536,128]{0,1:T(8,128)S(1)}, u32[]{:S(2)}, u32[]{:S(2)}) %collective-permute-start) | collective-permute-done | bytes 786464 | tf_op jit(solution)/shard_map/ppermute | solution.py:14
  136.4 3.9 fusion.62
  140.8 55.3 %all-reduce.7.cloned.1.call-done = f32[2,256,256]{2,1,0:T(8,128)} async-done(((f32[2,256,256]{2,1,0:T(8,128)}), f32[2,256,256]{2,1,0:T(8,128)}) %all-reduce.7.cloned.1.call-update) | async-done | bytes 524304 | tf_op jit(solution)/shard_map/psum | solution.py:45
  196.0 17.3 %copy.69 = f32[2,256,256]{0,2,1:T(8,128)} copy(f32[2,256,256]{2,1,0:T(8,128)} %all-reduce.7.cloned.1.call-done) | data formatting | bytes 1048576 | tf_op jit(solution)/shard_map/psum | solution.py:45
  213.3 3.0 gather_fusion.1
  220.2 1.9 fusion.21
  230.7 3.1 fusion.65
  235.8 16.9 %collective-permute-done.1 = f32[1536,128]{0,1:T(8,128)S(1)} collective-permute-done((f32[1536,128]{0,1:T(8,128)S(1)}, f32[1536,128]{0,1:T(8,128)S(1)}, u32[]{:S(2)}, u32[]{:S(2)}) %collective-permute-start.1) | collective-permute-done | bytes 786464 | tf_op jit(solution)/shard_map/ppermute | solution.py:14
  253.0 3.9 fusion.66
  257.0 55.7 %all-reduce.9.cloned.1.call-done = f32[2,256,256]{2,1,0:T(8,128)} async-done(((f32[2,256,256]{2,1,0:T(8,128)}), f32[2,256,256]{2,1,0:T(8,128)}) %all-reduce.9.cloned.1.call-update) | async-done | bytes 524304 | tf_op jit(solution)/shard_map/psum | solution.py:45
  312.6 17.3 %copy.76 = f32[2,256,256]{0,2,1:T(8,128)} copy(f32[2,256,256]{2,1,0:T(8,128)} %all-reduce.9.cloned.1.call-done) | data formatting | bytes 1048576 | tf_op jit(solution)/shard_map/psum | solution.py:45
  329.9 3.0 gather_fusion.2
  336.9 1.9 fusion.16
  347.4 3.1 fusion.69
  352.5 16.9 %collective-permute-done.2 = f32[1536,128]{0,1:T(8,128)S(1)} collective-permute-done((f32[1536,128]{0,1:T(8,128)S(1)}, f32[1536,128]{0,1:T(8,128)S(1)}, u32[]{:S(2)}, u32[]{:S(2)}) %collective-permute-start.2) | collective-permute-done | bytes 786464 | tf_op jit(solution)/shard_map/ppermute | solution.py:14
  369.7 3.9 fusion.70
  373.6 55.7 %all-reduce.11.cloned.1.call-done = f32[2,256,256]{2,1,0:T(8,128)} async-done(((f32[2,256,256]{2,1,0:T(8,128)}), f32[2,256,256]{2,1,0:T(8,128)}) %all-reduce.11.cloned.1.call-update) | async-done | bytes 524304 | tf_op jit(solution)/shard_map/psum | solution.py:45
  429.3 17.3 %copy.83 = f32[2,256,256]{0,2,1:T(8,128)} copy(f32[2,256,256]{2,1,0:T(8,128)} %all-reduce.11.cloned.1.call-done) | data formatting | bytes 1048576 | tf_op jit(solution)/shard_map/psum | solution.py:45
  446.6 3.0 gather_fusion.3
  453.5 1.9 fusion.11
  464.1 4.7 fusion.4
  468.8 13.7 %psum.39 = f32[512]{0:T(512)S(1)} all-reduce(f32[512]{0:T(512)S(1)} %bitcast.145), channel_id=1, replica_groups=mesh['rows'=8,'pairs'=4] {'rows'}, use_global_device_ids=true, to_apply=%region_9.10 | all-reduce | flops 512 | bytes 4096 | tf_op jit(solution)/shard_map/psum | solution.py:53
  482.5 2.2 bitcast_multiply_fusion
  484.7 74.3 %all_to_all.4 = f32[32,16,1536]{2,1,0:T(8,128)S(1)} all-to-all(f32[32,16,1536]{2,1,0:T(8,128)S(1)} %bitcast.135), channel_id=1, replica_groups=mesh['rows'=8,'pairs'=4] {'rows','pairs'}, dimensions={0} | all-to-all | bytes 6291456 | tf_op jit(solution)/shard_map/all_to_all | solution.py:61
  560.8 3.4 copy.102
  (89 shorter events, 60.0 us)
Async XLA Ops:
  6.5 70.5 %all-reduce.5.cloned.1.call-start = ((), (), s32[]{:S(2)}) async-start(), calls=%async_computation.1 | async-start | bytes 1048576 | tf_op jit(solution)/shard_map/psum | solution.py:45
  17.7 178.4 %all-reduce.7.cloned.1.call-start = ((), (), s32[]{:S(2)}) async-start(), calls=%async_computation.2 | async-start | bytes 1048576 | tf_op jit(solution)/shard_map/psum | solution.py:45
  100.1 3.3 copy-start
  100.1 3.9 copy-start.4
  117.6 18.5 %collective-permute-start = (f32[1536,128]{0,1:T(8,128)S(1)}, f32[1536,128]{0,1:T(8,128)S(1)}, u32[]{:S(2)}, u32[]{:S(2)}) collective-permute-start(f32[1536,128]{0,1:T(8,128)S(1)} %get-tuple-element.16), channel_id=1, source_target_pairs={{3,0},{0,1},{1,2},{2,3},{7,4},{4,5},{5,6},{6,7},{11,8},{8,9},{9,10... | collective-permute-start | bytes 2359304 | tf_op jit(solution)/shard_map/ppermute | solution.py:14
  140.2 172.4 %all-reduce.9.cloned.1.call-start = ((), (), s32[]{:S(2)}) async-start(), calls=%async_computation.3 | async-start | bytes 1048576 | tf_op jit(solution)/shard_map/psum | solution.py:45
  218.8 3.3 copy-start.1
  218.8 3.9 copy-start.5
  234.1 18.6 %collective-permute-start.1 = (f32[1536,128]{0,1:T(8,128)S(1)}, f32[1536,128]{0,1:T(8,128)S(1)}, u32[]{:S(2)}, u32[]{:S(2)}) collective-permute-start(f32[1536,128]{0,1:T(8,128)S(1)} %get-tuple-element.12), channel_id=1, source_target_pairs={{3,0},{0,1},{1,2},{2,3},{7,4},{4,5},{5,6},{6,7},{11,8},{8,9},{9,10... | collective-permute-start | bytes 2359304 | tf_op jit(solution)/shard_map/ppermute | solution.py:14
  256.9 172.4 %all-reduce.11.cloned.1.call-start = ((), (), s32[]{:S(2)}) async-start(), calls=%async_computation.4 | async-start | bytes 1048576 | tf_op jit(solution)/shard_map/psum | solution.py:45
  335.5 3.3 copy-start.2
  335.5 3.9 copy-start.6
  350.7 18.7 %collective-permute-start.2 = (f32[1536,128]{0,1:T(8,128)S(1)}, f32[1536,128]{0,1:T(8,128)S(1)}, u32[]{:S(2)}, u32[]{:S(2)}) collective-permute-start(f32[1536,128]{0,1:T(8,128)S(1)} %get-tuple-element.8), channel_id=1, source_target_pairs={{3,0},{0,1},{1,2},{2,3},{7,4},{4,5},{5,6},{6,7},{11,8},{8,9},{9,10... | collective-permute-start | bytes 2359304 | tf_op jit(solution)/shard_map/ppermute | solution.py:14
  452.1 3.3 copy-start.3
  452.1 3.9 copy-start.7
  464.0 18.4 %copy-start.8 = (f32[512]{0:T(512)S(1)}, f32[512]{0:T(512)}, u32[]{:S(2)}) copy-start(f32[512]{0:T(512)} %param.7) | copy-start | bytes 6148
Sparse Core Ops, SparseCore 0:
  17.8 59.2 all-reduce.4
  140.4 55.6 all-reduce.6
  257.0 55.5 all-reduce.8
  373.7 55.5 all-reduce.10
where the time goes:
time: 579 us; the launch traced here: 571 us
  waiting for transfers between devices  276 us (48%)
  local copies, waits for them, and re-layouts  91.6 us (16%)
  blocking collectives  88 us (15%)
  matrix products  75.5 us (13%)
  other arithmetic  20.6 us (4%)
  between operations  14 us (2%)
    psum x4, waiting for transfers between devices, on_device(): gram = lax.psum(partial_gram, 'rows')  225 us
    all_to_all x1, blocking collectives, on_device(): lax.all_to_all(packed, ('rows', 'pairs'), split_axis=0, concat_axis=1, ti...  74.3 us
    psum x4, local copies, waits for them, and re-layouts, on_device(): gram = lax.psum(partial_gram, 'rows')  69.3 us
    ppermute x3, waiting for transfers between devices, from_behind(): return lax.ppermute(block, axis, route)  50.8 us
    dot_general x4, matrix products, on_device(): partial_gram = jnp.einsum('rpi,rpj->pij', pairs, pairs, precision=HI)  17.7 us
    dot_general x12, matrix products, whitening_of(): jnp.einsum('pij,pjk->pik', zmat, ymat, precision=HI)  17.6 us
    dot_general x4, matrix products, on_device(): pairs = jnp.einsum('rpi,pij->rpj', pairs, whitening, precision=HI)  16.3 us
    dot_general x12, matrix products, whitening_of(): zmat = jnp.einsum('pij,pjk->pik', tmat, zmat, precision=HI)  15.2 us
  transfers between devices with their start and end apart: 7, of which 7 were waited for; matrix products, arithmetic and copies ran while one was open for 0% of the time, Pallas kernels for 0%

commit v1 on v0

--- a/solution.py
+++ b/solution.py
@@ -42,7 +42,9 @@
     for round_index in range(ROUNDS):
         pairs = filled.reshape(rows_here, 2, 2 * block)
         partial_gram = jnp.einsum("rpi,rpj->pij", pairs, pairs, precision=HI)
-        gram = lax.psum(partial_gram, "rows")
+        gram = partial_gram
+        for hop in (1, 2, 4):
+            gram = gram + lax.ppermute(gram, "rows", [(dev, dev ^ hop) for dev in range(8)])
         whitening = whitening_of(gram)
         pairs = jnp.einsum("rpi,pij->rpj", pairs, whitening, precision=HI)
         quads = pairs.reshape(rows_here, 4, block)

time: 579 us -> 520 us (0.90)
  waiting for transfers between devices: 276 us -> 204 us
  starting transfers between devices: 5.54 us -> 23.8 us
  between operations: 14 us -> 0.89 us
    psum x4 -> x0, waiting for transfers between devices: 225 us -> none  [on_device(): gram = lax.psum(partial_gram, 'rows')]
    ppermute x0 -> x12, waiting for transfers between devices: none -> 147 us  [on_device(): lax.ppermute(gram, 'rows', [(dev, dev ^ hop) for dev in range(8)])]
    add x0 -> x4, local copies, waits for them, and re-layouts: none -> 69.7 us  [on_device(): gram + lax.ppermute(gram, 'rows', [(dev, dev ^ hop) for dev in range(8)])]
    psum x4 -> x0, local copies, waits for them, and re-layouts: 69.3 us -> none  [on_device(): gram = lax.psum(partial_gram, 'rows')]
    ppermute x0 -> x12, starting transfers between devices: none -> 21.3 us  [on_device(): lax.ppermute(gram, 'rows', [(dev, dev ^ hop) for dev in range(8)])]
  transfers between devices with their start and end apart: 7 -> 15, of which waited for: 7 -> 15; matrix products, arithmetic and copies ran while one was open for 0% -> 0% of each run, Pallas kernels for 0% -> 0%
where the time goes in v1:
time: 520 us; the launch traced here: 511 us
  waiting for transfers between devices  204 us (39%)
  local copies, waits for them, and re-layouts  92 us (18%)
  blocking collectives  90.2 us (17%)
  matrix products  76.4 us (15%)
  other arithmetic  24.5 us (5%)
  starting transfers between devices  23.8 us (5%)
    ppermute x12, waiting for transfers between devices, on_device(): lax.ppermute(gram, 'rows', [(dev, dev ^ hop) for dev in range(8)])  147 us
    all_to_all x1, blocking collectives, on_device(): lax.all_to_all(packed, ('rows', 'pairs'), split_axis=0, concat_axis=1, ti...  73.5 us
    add x4, local copies, waits for them, and re-layouts, on_device(): gram + lax.ppermute(gram, 'rows', [(dev, dev ^ hop) for dev in range(8)])  69.7 us
    ppermute x3, waiting for transfers between devices, from_behind(): return lax.ppermute(block, axis, route)  56.4 us
    ppermute x12, starting transfers between devices, on_device(): lax.ppermute(gram, 'rows', [(dev, dev ^ hop) for dev in range(8)])  21.3 us
    dot_general x12, matrix products, whitening_of(): jnp.einsum('pij,pjk->pik', zmat, ymat, precision=HI)  17.6 us
    psum x1, blocking collectives, on_device(): squares = lax.psum(jnp.sum(filled * filled, axis=0), 'rows')  16.7 us
    dot_general x4, matrix products, on_device(): pairs = jnp.einsum('rpi,pij->rpj', pairs, whitening, precision=HI)  16.3 us
  transfers between devices with their start and end apart: 15, of which 15 were waited for; matrix products, arithmetic and copies ran while one was open for 0% of the time, Pallas kernels for 0%

profile of v1, /device:TPU:0, one launch (start us, length us, event | category | flops | bytes accessed | tf_op | source)
XLA Modules:
  0.0 511.5 jit_solution(43784975930515082)
XLA Ops:
  0.0 4.9 compare_select_fusion
  4.9 5.4 %fusion.2 = f32[2,256,256]{2,1,0:T(8,128)S(1)} fusion(f32[192,2,8,256]{3,2,1,0:T(8,128)S(1)} %bitcast.133), kind=kOutput, calls=%fused_computation.6 | convolution fusion | flops 2415919104 | bytes 3670016 | tf_op jit(solution)/shard_map/rpi,rpj->pij/dot_general | solution.py:44
  12.5 3.0 collective-permute-start.1
  15.5 12.2 %collective-permute-done.1 = f32[2,256,256]{2,1,0:T(8,128)S(1)} collective-permute-done((f32[2,256,256]{2,1,0:T(8,128)S(1)}, f32[2,256,256]{2,1,0:T(8,128)S(1)}, u32[]{:S(2)}, u32[]{:S(2)}) %collective-permute-start.1) | collective-permute-done | bytes 524320 | tf_op jit(solution)/shard_map/ppermute | solution.py:47
  31.3 22.0 %collective-permute-done.2 = f32[2,256,256]{2,1,0:T(8,128)S(1)} collective-permute-done((f32[2,256,256]{2,1,0:T(8,128)S(1)}, f32[2,256,256]{2,1,0:T(8,128)S(1)}, u32[]{:S(2)}, u32[]{:S(2)}) %collective-permute-start.2) | collective-permute-done | bytes 524320 | tf_op jit(solution)/shard_map/ppermute | solution.py:47
  54.2 17.5 %copy.62 = f32[2,256,256]{0,2,1:T(8,128)} copy(f32[2,256,256]{2,1,0:T(8,128)} %add.112) | data formatting | bytes 1048576 | tf_op jit(solution)/shard_map/add | solution.py:47
  71.7 3.0 gather_fusion
  90.1 5.3 %fusion = f32[2,256,1536]{2,1,0:T(8,128)S(1)} fusion(f32[2,256,256]{2,1,0:T(8,128)S(1)} %fusion.23, f32[192,2,8,256]{3,2,1,0:T(8,128)S(1)} %bitcast.134), kind=kOutput, calls=%fused_computation.4 | convolution fusion | flops 2415919104 | bytes 6815744 | tf_op jit(solution)/shard_map/rpi,pij->rpj/dot_general | solution.py:49
  97.2 18.1 %collective-permute-done.3 = f32[1536,128]{0,1:T(8,128)S(1)} collective-permute-done((f32[1536,128]{0,1:T(8,128)S(1)}, f32[1536,128]{0,1:T(8,128)S(1)}, u32[]{:S(2)}, u32[]{:S(2)}) %collective-permute-start.3) | collective-permute-done | bytes 786464 | tf_op jit(solution)/shard_map/ppermute | solution.py:14
  115.6 3.0 fusion.62
  122.2 12.5 %collective-permute-done.5 = f32[2,256,256]{2,1,0:T(8,128)S(1)} collective-permute-done((f32[2,256,256]{2,1,0:T(8,128)S(1)}, f32[2,256,256]{2,1,0:T(8,128)S(1)}, u32[]{:S(2)}, u32[]{:S(2)}) %collective-permute-start.5) | collective-permute-done | bytes 524320 | tf_op jit(solution)/shard_map/ppermute | solution.py:47
  134.8 3.2 collective-permute-start.6
  138.0 22.9 %collective-permute-done.6 = f32[2,256,256]{2,1,0:T(8,128)S(1)} collective-permute-done((f32[2,256,256]{2,1,0:T(8,128)S(1)}, f32[2,256,256]{2,1,0:T(8,128)S(1)}, u32[]{:S(2)}, u32[]{:S(2)}) %collective-permute-start.6) | collective-permute-done | bytes 524320 | tf_op jit(solution)/shard_map/ppermute | solution.py:47
  161.7 17.7 %copy.69 = f32[2,256,256]{0,2,1:T(8,128)} copy(f32[2,256,256]{2,1,0:T(8,128)} %add.116) | data formatting | bytes 1048576 | tf_op jit(solution)/shard_map/add | solution.py:47
  197.9 3.1 fusion.65
  202.1 18.9 %collective-permute-done.7 = f32[1536,128]{0,1:T(8,128)S(1)} collective-permute-done((f32[1536,128]{0,1:T(8,128)S(1)}, f32[1536,128]{0,1:T(8,128)S(1)}, u32[]{:S(2)}, u32[]{:S(2)}) %collective-permute-start.7) | collective-permute-done | bytes 786464 | tf_op jit(solution)/shard_map/ppermute | solution.py:14
  221.2 3.0 fusion.66
  228.0 12.3 %collective-permute-done.9 = f32[2,256,256]{2,1,0:T(8,128)S(1)} collective-permute-done((f32[2,256,256]{2,1,0:T(8,128)S(1)}, f32[2,256,256]{2,1,0:T(8,128)S(1)}, u32[]{:S(2)}, u32[]{:S(2)}) %collective-permute-start.9) | collective-permute-done | bytes 524320 | tf_op jit(solution)/shard_map/ppermute | solution.py:47
  240.4 3.3 collective-permute-start.10
  243.8 22.9 %collective-permute-done.10 = f32[2,256,256]{2,1,0:T(8,128)S(1)} collective-permute-done((f32[2,256,256]{2,1,0:T(8,128)S(1)}, f32[2,256,256]{2,1,0:T(8,128)S(1)}, u32[]{:S(2)}, u32[]{:S(2)}) %collective-permute-start.10) | collective-permute-done | bytes 524320 | tf_op jit(solution)/shard_map/ppermute | solution.py:47
  267.5 17.3 %copy.76 = f32[2,256,256]{0,2,1:T(8,128)} copy(f32[2,256,256]{2,1,0:T(8,128)} %add.120) | data formatting | bytes 1048576 | tf_op jit(solution)/shard_map/add | solution.py:47
  303.2 3.1 fusion.69
  306.9 19.4 %collective-permute-done.11 = f32[1536,128]{0,1:T(8,128)S(1)} collective-permute-done((f32[1536,128]{0,1:T(8,128)S(1)}, f32[1536,128]{0,1:T(8,128)S(1)}, u32[]{:S(2)}, u32[]{:S(2)}) %collective-permute-start.11) | collective-permute-done | bytes 786464 | tf_op jit(solution)/shard_map/ppermute | solution.py:14
  326.6 3.0 fusion.70
  333.4 12.3 %collective-permute-done.13 = f32[2,256,256]{2,1,0:T(8,128)S(1)} collective-permute-done((f32[2,256,256]{2,1,0:T(8,128)S(1)}, f32[2,256,256]{2,1,0:T(8,128)S(1)}, u32[]{:S(2)}, u32[]{:S(2)}) %collective-permute-start.13) | collective-permute-done | bytes 524320 | tf_op jit(solution)/shard_map/ppermute | solution.py:47
  345.8 3.3 collective-permute-start.14
  349.1 22.9 %collective-permute-done.14 = f32[2,256,256]{2,1,0:T(8,128)S(1)} collective-permute-done((f32[2,256,256]{2,1,0:T(8,128)S(1)}, f32[2,256,256]{2,1,0:T(8,128)S(1)}, u32[]{:S(2)}, u32[]{:S(2)}) %collective-permute-start.14) | collective-permute-done | bytes 524320 | tf_op jit(solution)/shard_map/ppermute | solution.py:47
  372.9 17.3 %copy.83 = f32[2,256,256]{0,2,1:T(8,128)} copy(f32[2,256,256]{2,1,0:T(8,128)} %add.124) | data formatting | bytes 1048576 | tf_op jit(solution)/shard_map/add | solution.py:47
  408.6 4.7 fusion.4
  413.4 16.7 %psum.7 = f32[512]{0:T(512)S(1)} all-reduce(f32[512]{0:T(512)S(1)} %bitcast.145), channel_id=1, replica_groups=mesh['rows'=8,'pairs'=4] {'rows'}, use_global_device_ids=true, to_apply=%region_5.6 | all-reduce | flops 512 | bytes 4096 | tf_op jit(solution)/shard_map/psum | solution.py:55
  432.2 73.5 %all_to_all.4 = f32[32,16,1536]{2,1,0:T(8,128)S(1)} all-to-all(f32[32,16,1536]{2,1,0:T(8,128)S(1)} %bitcast.135), channel_id=1, replica_groups=mesh['rows'=8,'pairs'=4] {'rows','pairs'}, dimensions={0} | all-to-all | bytes 6291456 | tf_op jit(solution)/shard_map/all_to_all | solution.py:63
  507.6 3.4 copy.102
  (105 shorter events, 99.2 us)
Async XLA Ops:
  10.3 2.1 collective-permute-start
  12.5 15.2 %collective-permute-start.1 = (f32[2,256,256]{2,1,0:T(8,128)S(1)}, f32[2,256,256]{2,1,0:T(8,128)S(1)}, u32[]{:S(2)}, u32[]{:S(2)}) collective-permute-start(f32[2,256,256]{2,1,0:T(8,128)S(1)} %add.110), channel_id=1, source_target_pairs={{0,8},{4,12},{8,0},{12,4},{16,24},{20,28},{24,16},{28,20},{1,9},{5... | collective-permute-start | bytes 1572872 | tf_op jit(solution)/shard_map/ppermute | solution.py:47
  27.8 25.6 %collective-permute-start.2 = (f32[2,256,256]{2,1,0:T(8,128)S(1)}, f32[2,256,256]{2,1,0:T(8,128)S(1)}, u32[]{:S(2)}, u32[]{:S(2)}) collective-permute-start(f32[2,256,256]{2,1,0:T(8,128)S(1)} %add.111), channel_id=1, source_target_pairs={{0,16},{4,20},{8,24},{12,28},{16,0},{20,4},{24,8},{28,12},{1,17},{... | collective-permute-start | bytes 1572872 | tf_op jit(solution)/shard_map/ppermute | solution.py:47
  77.2 5.0 copy-start
  95.8 19.5 %collective-permute-start.3 = (f32[1536,128]{0,1:T(8,128)S(1)}, f32[1536,128]{0,1:T(8,128)S(1)}, u32[]{:S(2)}, u32[]{:S(2)}) collective-permute-start(f32[1536,128]{0,1:T(8,128)S(1)} %get-tuple-element.16), channel_id=1, source_target_pairs={{3,0},{0,1},{1,2},{2,3},{7,4},{4,5},{5,6},{6,7},{11,8},{8,9},{9,10... | collective-permute-start | bytes 2359304 | tf_op jit(solution)/shard_map/ppermute | solution.py:14
  118.6 2.0 collective-permute-start.4
  120.7 14.0 %collective-permute-start.5 = (f32[2,256,256]{2,1,0:T(8,128)S(1)}, f32[2,256,256]{2,1,0:T(8,128)S(1)}, u32[]{:S(2)}, u32[]{:S(2)}) collective-permute-start(f32[2,256,256]{2,1,0:T(8,128)S(1)} %add.114), channel_id=1, source_target_pairs={{0,8},{4,12},{8,0},{12,4},{16,24},{20,28},{24,16},{28,20},{1,9},{5... | collective-permute-start | bytes 1572872 | tf_op jit(solution)/shard_map/ppermute | solution.py:47
  134.8 26.0 %collective-permute-start.6 = (f32[2,256,256]{2,1,0:T(8,128)S(1)}, f32[2,256,256]{2,1,0:T(8,128)S(1)}, u32[]{:S(2)}, u32[]{:S(2)}) collective-permute-start(f32[2,256,256]{2,1,0:T(8,128)S(1)} %add.115), channel_id=1, source_target_pairs={{0,16},{4,20},{8,24},{12,28},{16,0},{20,4},{24,8},{28,12},{1,17},{... | collective-permute-start | bytes 1572872 | tf_op jit(solution)/shard_map/ppermute | solution.py:47
  185.0 5.0 copy-start.1
  201.2 19.7 %collective-permute-start.7 = (f32[1536,128]{0,1:T(8,128)S(1)}, f32[1536,128]{0,1:T(8,128)S(1)}, u32[]{:S(2)}, u32[]{:S(2)}) collective-permute-start(f32[1536,128]{0,1:T(8,128)S(1)} %get-tuple-element.12), channel_id=1, source_target_pairs={{3,0},{0,1},{1,2},{2,3},{7,4},{4,5},{5,6},{6,7},{11,8},{8,9},{9,10... | collective-permute-start | bytes 2359304 | tf_op jit(solution)/shard_map/ppermute | solution.py:14
  224.3 2.0 collective-permute-start.8
  226.3 14.0 %collective-permute-start.9 = (f32[2,256,256]{2,1,0:T(8,128)S(1)}, f32[2,256,256]{2,1,0:T(8,128)S(1)}, u32[]{:S(2)}, u32[]{:S(2)}) collective-permute-start(f32[2,256,256]{2,1,0:T(8,128)S(1)} %add.118), channel_id=1, source_target_pairs={{0,8},{4,12},{8,0},{12,4},{16,24},{20,28},{24,16},{28,20},{1,9},{5... | collective-permute-start | bytes 1572872 | tf_op jit(solution)/shard_map/ppermute | solution.py:47
  240.4 26.2 %collective-permute-start.10 = (f32[2,256,256]{2,1,0:T(8,128)S(1)}, f32[2,256,256]{2,1,0:T(8,128)S(1)}, u32[]{:S(2)}, u32[]{:S(2)}) collective-permute-start(f32[2,256,256]{2,1,0:T(8,128)S(1)} %add.119), channel_id=1, source_target_pairs={{0,16},{4,20},{8,24},{12,28},{16,0},{20,4},{24,8},{28,12},{1,17},{... | collective-permute-start | bytes 1572872 | tf_op jit(solution)/shard_map/ppermute | solution.py:47
  290.3 5.0 copy-start.2
  306.6 19.7 %collective-permute-start.11 = (f32[1536,128]{0,1:T(8,128)S(1)}, f32[1536,128]{0,1:T(8,128)S(1)}, u32[]{:S(2)}, u32[]{:S(2)}) collective-permute-start(f32[1536,128]{0,1:T(8,128)S(1)} %get-tuple-element.8), channel_id=1, source_target_pairs={{3,0},{0,1},{1,2},{2,3},{7,4},{4,5},{5,6},{6,7},{11,8},{8,9},{9,10... | collective-permute-start | bytes 2359304 | tf_op jit(solution)/shard_map/ppermute | solution.py:14
  329.7 2.0 collective-permute-start.12
  331.7 14.0 %collective-permute-start.13 = (f32[2,256,256]{2,1,0:T(8,128)S(1)}, f32[2,256,256]{2,1,0:T(8,128)S(1)}, u32[]{:S(2)}, u32[]{:S(2)}) collective-permute-start(f32[2,256,256]{2,1,0:T(8,128)S(1)} %add.122), channel_id=1, source_target_pairs={{0,8},{4,12},{8,0},{12,4},{16,24},{20,28},{24,16},{28,20},{1,9},{5... | collective-permute-start | bytes 1572872 | tf_op jit(solution)/shard_map/ppermute | solution.py:47
  345.8 26.2 %collective-permute-start.14 = (f32[2,256,256]{2,1,0:T(8,128)S(1)}, f32[2,256,256]{2,1,0:T(8,128)S(1)}, u32[]{:S(2)}, u32[]{:S(2)}) collective-permute-start(f32[2,256,256]{2,1,0:T(8,128)S(1)} %add.123), channel_id=1, source_target_pairs={{0,16},{4,20},{8,24},{12,28},{16,0},{20,4},{24,8},{28,12},{1,17},{... | collective-permute-start | bytes 1572872 | tf_op jit(solution)/shard_map/ppermute | solution.py:47
  395.7 5.0 copy-start.3
  408.6 21.5 %copy-start.4 = (f32[512]{0:T(512)S(1)}, f32[512]{0:T(512)}, u32[]{:S(2)}) copy-start(f32[512]{0:T(512)} %param.7) | copy-start | bytes 6148
